TPU v7x, 512 devices: a whole 4x4x16 slice. The times are simulated.
512 devices in a mesh: blk: 256 (over x, y_hi, z, core), tgt: 2 (over y_lo).
Axes of the slice: x: 4, y: 4 (y_hi: 2, y_lo: 2; y = y_hi * 2 + y_lo), z: 16, core: 2. Of those that a mesh axis runs over, the one named last changes fastest.
Arguments:
- gradients: bfloat16 [131072, 8192], P('blk', 'tgt'), may hold values from -6 to 6
- targets: bfloat16 [131072, 64], P('blk'), may hold values from -0.15625 to 0.15625
Outputs:
- kernel_tiles: bfloat16 [3, 131072, 512], P(None, ('blk', 'tgt'))
- influence: float32 [131072, 64], P(('blk', 'tgt'))
All inputs are finite; a program needn't handle non-finite values.
Results may differ from a plain program's by a relative error of at most 0.0029.
Values may be sent and summed in bfloat16 or wider, within the bound.
A program may use at most 64 MiB of HBM per device.

v0:
```python
import jax
import jax.numpy as jnp
from jax import lax
from jax.sharding import PartitionSpec as P

P_SIZE = 8192
ROUNDS = 2


def from_partner(block, axis, stride):
    count = lax.axis_size(axis)
    route = []
    for low in range(count):
        high = low | 1 << stride
        if high != low and high < count:
            route += [(low, high), (high, low)]
    return lax.ppermute(block, axis, route)


def contract(left, right):
    return lax.dot_general(
        left, right, (((1,), (1,)), ((), ())), preferred_element_type=jnp.float32
    )


def per_device(gradients, targets):
    scale = 1.0 / P_SIZE**0.5
    levels = list(range(ROUNDS))
    tile_map = {}
    self_summed = lax.psum_scatter(
        contract(gradients, gradients), "tgt", scatter_dimension=0, tiled=True
    )
    self_tile = (self_summed * scale).astype(jnp.bfloat16)
    influence = jnp.dot(self_tile, targets, preferred_element_type=jnp.float32)
    for level in levels:
        opponent_grads, opponent_targets = from_partner((gradients, targets), "blk", level)
        partial_value = contract(gradients, opponent_grads)
        summed = lax.psum_scatter(partial_value, "tgt", scatter_dimension=0, tiled=True)
        tile = (summed * scale).astype(jnp.bfloat16)
        tile_map[level] = tile
        influence = influence + jnp.dot(tile, opponent_targets, preferred_element_type=jnp.float32)
    kernel_tiles = jnp.stack([self_tile] + [tile_map[level] for level in range(ROUNDS)], 0)
    return (kernel_tiles, influence)


def solution(mesh):
    placed = (P("blk", "tgt"), P("blk", None))
    return jax.shard_map(
        per_device,
        mesh=mesh,
        in_specs=placed,
        out_specs=(P(None, ("blk", "tgt"), None), P(("blk", "tgt"), None)),
        check_vma=False,
    )
```

profile of v0, /device:TPU:1, one launch (start us, length us, event | category | flops | bytes accessed | tf_op | source)
XLA Modules:
  0.0 158.8 jit_solution(5781544538134089059)
XLA Ops:
  7.2 0.0 reduce-scatter.4.cloned.1.call-start
  7.2 8.8 %collective-permute-start = (bf16[512,4096]{1,0:T(8,128)(2,1)}, bf16[512,4096]{1,0:T(8,128)(2,1)}, u32[]{:S(2)}, u32[]{:S(2)}) collective-permute-start(bf16[512,4096]{1,0:T(8,128)(2,1)} %param.2), channel_id=1, source_target_pairs={{0,2},{2,0},{4,6},{6,4},{8,10},{10,8},{12,14},{14,12},{16,18},{18,... | collective-permute-start | bytes 12582920 | tf_op jit(solution)/shard_map/ppermute | solution.py:17
  16.0 1.9 %collective-permute-start.1 = (bf16[512,4096]{1,0:T(8,128)(2,1)}, bf16[512,4096]{1,0:T(8,128)(2,1)}, u32[]{:S(2)}, u32[]{:S(2)}) collective-permute-start(bf16[512,4096]{1,0:T(8,128)(2,1)} %param.2), channel_id=1, source_target_pairs={{0,4},{4,0},{2,6},{6,2},{8,12},{12,8},{10,14},{14,10},{16,20},{20,... | collective-permute-start | bytes 12582920 | tf_op jit(solution)/shard_map/ppermute | solution.py:17
  17.9 6.8 %fusion.7 = f32[512,512]{1,0:T(8,128)} fusion(bf16[512,4096]{1,0:T(8,128)(2,1)} %param.2), kind=kOutput, calls=%fused_computation.13 | convolution fusion | flops 2147483648 | bytes 5242880 | tf_op jit(solution)/shard_map/dot_general | solution.py:21
  24.7 0.0 reduce-scatter.4.cloned.1.call-update
  24.7 0.0 reduce-scatter.6.cloned.1.call-start
  24.8 0.0 collective-permute-done
  24.8 6.9 %fusion.8 = f32[512,512]{1,0:T(8,128)} fusion(bf16[512,4096]{1,0:T(8,128)(2,1)} %param.2, bf16[512,4096]{1,0:T(8,128)(2,1)} %collective-permute-done), kind=kOutput, calls=%fused_computation.14 | convolution fusion | flops 2147483648 | bytes 9437184 | tf_op jit(solution)/shard_map/dot_general | solution.py:21
  31.6 0.0 reduce-scatter.6.cloned.1.call-update
  31.7 0.0 copy-start
  31.7 0.0 reduce-scatter.8.cloned.1.call-start
  31.7 78.6 %collective-permute-done.1 = bf16[512,4096]{1,0:T(8,128)(2,1)} collective-permute-done((bf16[512,4096]{1,0:T(8,128)(2,1)}, bf16[512,4096]{1,0:T(8,128)(2,1)}, u32[]{:S(2)}, u32[]{:S(2)}) %collective-permute-start.1) | collective-permute-done | bytes 4194336 | tf_op jit(solution)/shard_map/ppermute | solution.py:17
  110.3 6.8 %fusion.9 = f32[512,512]{1,0:T(8,128)} fusion(bf16[512,4096]{1,0:T(8,128)(2,1)} %param.2, bf16[512,4096]{1,0:T(8,128)(2,1)} %collective-permute-done.1), kind=kOutput, calls=%fused_computation.15 | convolution fusion | flops 2147483648 | bytes 9437184 | tf_op jit(solution)/shard_map/dot_general | solution.py:21
  117.1 0.0 reduce-scatter.8.cloned.1.call-update
  117.1 0.0 copy-done
  117.1 2.2 %collective-permute-start.3 = (bf16[512,64]{0,1:T(8,128)(2,1)S(1)}, bf16[512,64]{0,1:T(8,128)(2,1)S(1)}, u32[]{:S(2)}, u32[]{:S(2)}) collective-permute-start(bf16[512,64]{0,1:T(8,128)(2,1)S(1)} %copy-done), channel_id=1, source_target_pairs={{0,4},{4,0},{2,6},{6,2},{8,12},{12,8},{10,14},{14,10},{16,20},{20,... | collective-permute-start | bytes 196616 | tf_op jit(solution)/shard_map/ppermute | solution.py:17
  119.3 2.8 %collective-permute-start.2 = (bf16[512,64]{0,1:T(8,128)(2,1)S(1)}, bf16[512,64]{0,1:T(8,128)(2,1)S(1)}, u32[]{:S(2)}, u32[]{:S(2)}) collective-permute-start(bf16[512,64]{0,1:T(8,128)(2,1)S(1)} %copy-done), channel_id=1, source_target_pairs={{0,2},{2,0},{4,6},{6,4},{8,10},{10,8},{12,14},{14,12},{16,18},{18,... | collective-permute-start | bytes 196616 | tf_op jit(solution)/shard_map/ppermute | solution.py:17
  122.1 0.0 reduce-scatter.4.cloned.1.call-done
  122.2 1.2 fusion
  123.4 1.1 fusion.1
  124.5 0.0 reduce-scatter.6.cloned.1.call-done
  124.5 1.1 fusion.2
  125.6 21.4 %reduce-scatter.8.cloned.1.call-done = f32[256,512]{1,0:T(8,128)} async-done(((f32[512,512]{1,0:T(8,128)}), f32[256,512]{1,0:T(8,128)}) %reduce-scatter.8.cloned.1.call-update) | async-done | bytes 524304 | tf_op jit(solution)/shard_map/reduce_scatter | solution.py:38
  147.0 1.1 fusion.3
  148.1 0.0 collective-permute-done.2
  148.1 1.3 convolution_add_fusion.1
  149.4 1.0 pad_maximum_fusion
  150.4 0.0 collective-permute-done.3
  150.4 1.9 %convolution_add_fusion = f32[256,64]{0,1:T(8,128)} fusion(f32[256,64]{0,1:T(8,128)S(1)} %convolution_add_fusion.1, bf16[512,64]{0,1:T(8,128)(2,1)S(1)} %collective-permute-done.3, f32[256,512]{1,0:T(8,128)} %reduce-scatter.8.cloned.1.call-done), kind=kOutput, calls=%fused_computation | convolution fusion | flops 17055744 | bytes 720896 | tf_op jit(solution)/shard_map/dot_general | solution.py:41
Async XLA Ops:
  7.2 115.0 %reduce-scatter.4.cloned.1.call-start = ((), (), s32[]{:S(2)}) async-start(), calls=%async_computation.3 | async-start | bytes 1572864 | tf_op jit(solution)/shard_map/reduce_scatter | solution.py:30
  7.2 17.6 %collective-permute-start = (bf16[512,4096]{1,0:T(8,128)(2,1)}, bf16[512,4096]{1,0:T(8,128)(2,1)}, u32[]{:S(2)}, u32[]{:S(2)}) collective-permute-start(bf16[512,4096]{1,0:T(8,128)(2,1)} %param.2), channel_id=1, source_target_pairs={{0,2},{2,0},{4,6},{6,4},{8,10},{10,8},{12,14},{14,12},{16,18},{18,... | collective-permute-start | bytes 12582920 | tf_op jit(solution)/shard_map/ppermute | solution.py:17
  16.0 94.3 %collective-permute-start.1 = (bf16[512,4096]{1,0:T(8,128)(2,1)}, bf16[512,4096]{1,0:T(8,128)(2,1)}, u32[]{:S(2)}, u32[]{:S(2)}) collective-permute-start(bf16[512,4096]{1,0:T(8,128)(2,1)} %param.2), channel_id=1, source_target_pairs={{0,4},{4,0},{2,6},{6,2},{8,12},{12,8},{10,14},{14,10},{16,20},{20,... | collective-permute-start | bytes 12582920 | tf_op jit(solution)/shard_map/ppermute | solution.py:17
  24.7 99.8 %reduce-scatter.6.cloned.1.call-start = ((), (), s32[]{:S(2)}) async-start(), calls=%async_computation.4 | async-start | bytes 1572864 | tf_op jit(solution)/shard_map/reduce_scatter | solution.py:38
  31.7 85.5 %copy-start = (bf16[512,64]{0,1:T(8,128)(2,1)S(1)}, bf16[512,64]{0,1:T(8,128)(2,1)}, u32[]{:S(2)}) copy-start(bf16[512,64]{0,1:T(8,128)(2,1)} %param.3) | copy-start | bytes 196612
  31.7 115.4 %reduce-scatter.8.cloned.1.call-start = ((), (), s32[]{:S(2)}) async-start(), calls=%async_computation.5 | async-start | bytes 1572864 | tf_op jit(solution)/shard_map/reduce_scatter | solution.py:38
  117.1 33.2 %collective-permute-start.3 = (bf16[512,64]{0,1:T(8,128)(2,1)S(1)}, bf16[512,64]{0,1:T(8,128)(2,1)S(1)}, u32[]{:S(2)}, u32[]{:S(2)}) collective-permute-start(bf16[512,64]{0,1:T(8,128)(2,1)S(1)} %copy-done), channel_id=1, source_target_pairs={{0,4},{4,0},{2,6},{6,2},{8,12},{12,8},{10,14},{14,10},{16,20},{20,... | collective-permute-start | bytes 196616 | tf_op jit(solution)/shard_map/ppermute | solution.py:17
  119.3 28.8 %collective-permute-start.2 = (bf16[512,64]{0,1:T(8,128)(2,1)S(1)}, bf16[512,64]{0,1:T(8,128)(2,1)S(1)}, u32[]{:S(2)}, u32[]{:S(2)}) collective-permute-start(bf16[512,64]{0,1:T(8,128)(2,1)S(1)} %copy-done), channel_id=1, source_target_pairs={{0,2},{2,0},{4,6},{6,4},{8,10},{10,8},{12,14},{14,12},{16,18},{18,... | collective-permute-start | bytes 196616 | tf_op jit(solution)/shard_map/ppermute | solution.py:17
Sparse Core Ops, SparseCore 0:
  24.8 29.8 reduce-scatter.3
  57.5 31.6 reduce-scatter.5
  117.2 29.7 reduce-scatter.7
where the time goes:
time: 159 us
  waiting for transfers between devices  100 us (63%)
  matrix products  24.8 us (16%)
  starting transfers between devices  15.8 us (10%)
  between operations  13.8 us (9%)
  other arithmetic  4.23 us (3%)
    ppermute x4, waiting for transfers between devices, from_partner(): return lax.ppermute(block, axis, route)  78.6 us
    reduce_scatter x2, waiting for transfers between devices, per_device(): lax.psum_scatter(partial_value, 'tgt', scatter_dimension=0, tiled=True)  21.4 us
    dot_general x3, matrix products, contract(): lax.dot_general(left, right, (((1,), (1,)), ((), ())), preferred_element_...  20.5 us
    ppermute x4, starting transfers between devices, from_partner(): return lax.ppermute(block, axis, route)  15.7 us
    another operation x4, other arithmetic, per_device(): jnp.stack([self_tile] + [tile_map[level] for level in range(ROUNDS)], 0)  4.23 us
  transfers between devices with their start and end apart: 7, of which 2 were waited for; matrix products, arithmetic and copies ran while one was open for 17% of the time, Pallas kernels for 0%

commit v1 on v0

v1 whole, which is shorter than its diff:
```python
import functools

import jax
import jax.numpy as jnp
from jax import lax
from jax.experimental import pallas as pl
from jax.experimental.pallas import tpu as pltpu
from jax.sharding import PartitionSpec as P

MESH = pl.DeviceIdType.MESH
NT = (((1,), (1,)), ((), ()))
HALF_GROUPS = ((0, 128), (128, 64), (192, 64))
LAST_PIECES = 4
STEP = 1024


def chunk_list(half, features):
    groups = [(h * half + start, rows) for h in range(2) for start, rows in HALF_GROUPS]
    chunks = []
    for index, (start, rows) in enumerate(groups):
        pieces = LAST_PIECES if index == len(groups) - 1 else 1
        width = features // pieces
        chunks.append([(start, rows, at * width, width) for at in range(pieces)])
    return groups, chunks


def kernel(
    scale,
    grads_hbm, targ_hbm, tiles_hbm, infl_hbm,
    own, other, targ, packed, packed_in, self_out, self_in, self_keep, self_tile,
    part_out, part_in, part_keep, staged, mine, result, infl,
    own_sem, targ_sem, grad_send, grad_recv, pack_send, pack_recv, self_send, self_recv,
    part_send, part_recv, res_send, res_recv, out_sem,
):
    rows, features = grads_hbm.shape
    half = rows // 2
    blk, y = lax.axis_index("blk"), lax.axis_index("tgt")
    core, z = lax.rem(blk, 2), lax.rem(blk // 2, 2)
    chip_blk, z_blk = blk + 1 - 2 * core, blk + 2 - 4 * z
    role = lax.rem(core + z, 2)
    sink = chip_blk + role * (z_blk - chip_blk)
    src = z_blk + role * (chip_blk - z_blk)
    slot_made, slot_got = 2 - role, 1 + role
    y_other = 1 - y
    groups, chunks = chunk_list(half, features)
    per_half = len(HALF_GROUPS)

    def there(block, side):
        return {"blk": block, "tgt": side}

    def half_rows(side):
        return pl.ds(pl.multiple_of(side * half, half), half)

    load_own = pltpu.make_async_copy(grads_hbm, own, own_sem)
    load_own.start()
    load_targ = pltpu.make_async_copy(targ_hbm, targ, targ_sem)
    load_targ.start()

    barrier = pltpu.get_barrier_semaphore()
    for peer in (there(chip_blk, y), there(z_blk, y), there(blk, y_other), there(z_blk, y_other), there(chip_blk, y_other)):
        pl.semaphore_signal(barrier, inc=1, device_id=peer, device_id_type=MESH)
    pl.semaphore_wait(barrier, 5)

    def remote(source, target, send, recv, device):
        return pltpu.make_async_remote_copy(
            src_ref=source, dst_ref=target, send_sem=send, recv_sem=recv, device_id=device, device_id_type=MESH
        )

    grad_copies = []
    for pieces in chunks:
        for start, count, first, width in pieces:
            at = len(grad_copies)
            where = (pl.ds(start, count), pl.ds(first, width))
            copy = remote(grads_hbm.at[where], other.at[where], grad_send.at[at], grad_recv.at[at], there(sink, y))
            copy.start()
            grad_copies.append(copy)

    def contract(left, left_rows, right_rows, first, width, init):
        def body(k, total):
            cols = pl.ds(pl.multiple_of(first + k * STEP, STEP), STEP)
            return total + lax.dot_general(
                left[left_rows, cols], own[right_rows, cols], NT, preferred_element_type=jnp.float32
            )

        return lax.fori_loop(0, width // STEP, body, init)

    load_own.wait()
    zero = jnp.zeros((128, half), jnp.float32)
    for into, side in ((self_out, y_other), (self_keep, y)):
        for r in range(half // 128):
            left_rows = pl.ds(pl.multiple_of(side * half + r * 128, 128), 128)
            for n in range(2):
                into[pl.ds(r * 128, 128), pl.ds(n * half, half)] = contract(
                    own, left_rows, pl.ds(n * half, half), 0, features, zero
                )
        if into is self_out:
            self_copy = remote(self_out, self_in, self_send, self_recv, there(blk, y_other))
            self_copy.start()

    load_targ.wait()
    packed[:, : targ.shape[1]] = targ[pl.ds(0, half), :]
    packed[:, targ.shape[1] :] = targ[pl.ds(half, half), :]

    part_copies = [
        remote(
            part_out.at[pl.ds(start, count)], part_in.at[pl.ds(start, count)],
            part_send.at[g], part_recv.at[g], there(blk, y_other),
        )
        for g, (start, count) in enumerate(groups)
    ]
    res_copies = [
        remote(
            staged.at[pl.ds(start, count)], result.at[y, pl.ds(start % half, count)],
            res_send.at[g], res_recv.at[y, g % per_half], there(src, g // per_half),
        )
        for g, (start, count) in enumerate(groups)
    ]

    def finish(g):
        start, count = groups[g]
        part_copies[g].wait_recv()
        here = pl.ds(start, count)
        staged[here, :] = ((part_keep[here, :] + part_in[here, :]) * scale).astype(jnp.bfloat16)

    def turn(g):
        end = groups[g][0] + groups[g][1]
        if end % 128 == 0:
            here = pl.ds(end - 128, 128)
            block = (part_keep[here, :] + part_in[here, :]) * scale
            mine[:, end - 128 : end] = block.T.astype(jnp.bfloat16)

    at = 0
    for g, (start, count) in enumerate(groups):
        here = pl.ds(start, count)
        for piece, (_, _, first, width) in enumerate(chunks[g]):
            grad_copies[at].wait_recv()
            at += 1
            zeros = jnp.zeros((count, half), jnp.float32)
            last = piece == len(chunks[g]) - 1
            for into, side in ((part_out, y_other), (part_keep, y)):
                into[here, :] = contract(
                    other, here, half_rows(side), first, width, zeros if piece == 0 else into[here, :]
                )
                if last and into is part_out:
                    part_copies[g].start()
        if g >= 1:
            finish(g - 1)
            turn(g - 1)
        if g == 0:
            self_copy.wait_recv()
            self_tile[...] = ((self_keep[...] + self_in[...]) * scale).astype(jnp.bfloat16)
            put_self = pltpu.make_async_copy(self_tile, tiles_hbm.at[0], out_sem.at[0])
            put_self.start()

    for copy in res_copies[:-1]:
        copy.start()
    pack_copies = [
        remote(packed, packed_in.at[1], pack_send.at[0], pack_recv.at[1], there(src, y)),
        remote(packed, packed_in.at[0], pack_send.at[1], pack_recv.at[0], there(sink, y)),
    ]
    for copy in pack_copies:
        copy.start()

    finish(len(groups) - 1)
    res_copies[-1].start()

    turn(len(groups) - 1)
    put_mine = pltpu.make_async_copy(mine, tiles_hbm.at[slot_made], out_sem.at[1])
    put_mine.start()

    def influence_of(left, right, weights):
        width = weights.shape[1] // 2
        return (
            jnp.dot(left, weights, preferred_element_type=jnp.float32)[:, :width]
            + jnp.dot(right, weights, preferred_element_type=jnp.float32)[:, width:]
        )

    total = influence_of(self_tile[:, :half], self_tile[:, half:], packed[...])
    for copy in pack_copies:
        copy.wait_recv()
    total = total + influence_of(mine[:, :half], mine[:, half:], packed_in[0])
    for side in range(2):
        for k, (start, count) in enumerate(HALF_GROUPS):
            landed = result.at[side, pl.ds(start, count)]
            remote(staged.at[pl.ds(start, count)], landed, res_send.at[k], res_recv.at[side, k], there(sink, y)).wait_recv()
    puts = [
        pltpu.make_async_copy(
            result.at[side], tiles_hbm.at[slot_got, :, pl.ds(side * half, half)], out_sem.at[2 + side]
        )
        for side in range(2)
    ]
    for put in puts:
        put.start()
    total = total + influence_of(result[0], result[1], packed_in[1])
    infl[...] = total
    put_infl = pltpu.make_async_copy(infl, infl_hbm, out_sem.at[4])
    put_infl.start()

    for copy in grad_copies + part_copies + res_copies + pack_copies + [self_copy]:
        copy.wait_send()
    for put in [put_self, put_mine, put_infl] + puts:
        put.wait()


def per_device(gradients, targets):
    rows, features = gradients.shape
    half, columns = rows // 2, targets.shape[1]
    groups, chunks = chunk_list(half, features)
    count = sum(len(pieces) for pieces in chunks)
    bf16, f32 = jnp.bfloat16, jnp.float32
    dma = pltpu.SemaphoreType.DMA
    return pl.pallas_call(
        functools.partial(kernel, 1.0 / (2 * features) ** 0.5),
        out_shape=(
            jax.ShapeDtypeStruct((3, half, rows), bf16),
            jax.ShapeDtypeStruct((half, columns), f32),
        ),
        in_specs=[pl.BlockSpec(memory_space=pl.ANY)] * 2,
        out_specs=[pl.BlockSpec(memory_space=pl.ANY)] * 2,
        scratch_shapes=[
            pltpu.VMEM((rows, features), bf16),
            pltpu.VMEM((rows, features), bf16),
            pltpu.VMEM((rows, columns), bf16),
            pltpu.VMEM((half, 2 * columns), bf16),
            pltpu.VMEM((2, half, 2 * columns), bf16),
            pltpu.VMEM((half, rows), f32),
            pltpu.VMEM((half, rows), f32),
            pltpu.VMEM((half, rows), f32),
            pltpu.VMEM((half, rows), bf16),
            pltpu.VMEM((rows, half), f32),
            pltpu.VMEM((rows, half), f32),
            pltpu.VMEM((rows, half), f32),
            pltpu.VMEM((rows, half), bf16),
            pltpu.VMEM((half, rows), bf16),
            pltpu.VMEM((2, half, half), bf16),
            pltpu.VMEM((half, columns), f32),
            dma, dma, dma((count,)), dma((count,)), dma((2,)), dma((2,)), dma, dma,
            dma((len(groups),)), dma((len(groups),)), dma((len(groups),)), dma((2, len(HALF_GROUPS))), dma((5,)),
        ],
        compiler_params=pltpu.CompilerParams(collective_id=0, has_side_effects=True),
    )(gradients, targets)


def solution(mesh):
    placed = (P("blk", "tgt"), P("blk", None))
    return jax.shard_map(
        per_device,
        mesh=mesh,
        in_specs=placed,
        out_specs=(P(None, ("blk", "tgt"), None), P(("blk", "tgt"), None)),
        check_vma=False,
    )
```

time: 159 us -> 68.7 us (0.43)
  waiting for transfers between devices: 100 us -> 0 us
  Pallas kernels: 0 us -> 62.1 us
  matrix products: 24.8 us -> 0 us
  starting transfers between devices: 15.8 us -> 0 us
  between operations: 13.8 us -> 0.64 us
  local copies, waits for them, and re-layouts: 0.01 us -> 5.28 us
  other arithmetic: 4.23 us -> 0 us
    ppermute x4 -> x0, waiting for transfers between devices: 78.6 us -> none  [from_partner(): return lax.ppermute(block, axis, route)]
    pallas_call x0 -> x1, Pallas kernels: none -> 62.1 us  [per_device(): pl.pallas_call(functools.partial(kernel, 1.0 / (2 * features) ** 0.5), ou...]
    dot_general x6 -> x0, matrix products: 24.8 us -> none  [the longest x3 20.5 us: contract(): lax.dot_general(left, right, (((1,), (1,)), ((), ())), preferred_element_...]
    reduce_scatter x3 -> x0, waiting for transfers between devices: 21.5 us -> none  [the longest x2 21.4 us: per_device(): lax.psum_scatter(partial_value, 'tgt', scatter_dimension=0, tiled=True)]
    ppermute x4 -> x0, starting transfers between devices: 15.7 us -> none  [from_partner(): return lax.ppermute(block, axis, route)]
    another operation x4 -> x0, other arithmetic: 4.23 us -> none  [per_device(): jnp.stack([self_tile] + [tile_map[level] for level in range(ROUNDS)], 0)]
    unnamed x2, local copies, waits for them, and re-layouts: 0.01 us -> 3.66 us
    pallas_call x0 -> x1, local copies, waits for them, and re-layouts: none -> 1.62 us  [per_device(): pl.pallas_call(functools.partial(kernel, 1.0 / (2 * features) ** 0.5), ou...]
  transfers between devices with their start and end apart: 7 -> 0, of which waited for: 2 -> 0; matrix products, arithmetic and copies ran while one was open for 17% -> 0% of each run, Pallas kernels for 0% -> 0%
where the time goes in v1:
time: 68.7 us; the launch traced here: 68 us
  Pallas kernels  62.1 us (90%)
  local copies, waits for them, and re-layouts  5.28 us (8%)
    pallas_call x1, Pallas kernels, per_device(): pl.pallas_call(functools.partial(kernel, 1.0 / (2 * features) ** 0.5), ou...  62.1 us
    unnamed x2, local copies, waits for them, and re-layouts  3.66 us
    pallas_call x1, local copies, waits for them, and re-layouts, per_device(): pl.pallas_call(functools.partial(kernel, 1.0 / (2 * features) ** 0.5), ou...  1.62 us

profile of v1, /device:TPU:1, one launch (start us, length us, event | category | flops | bytes accessed | tf_op | source)
XLA Modules:
  0.0 68.0 jit_solution(1162330559174343064)
XLA Ops:
  0.6 1.6 %copy.4.targ_hbm = bf16[512,64]{1,0:T(8,128)(2,1)} copy(bf16[512,64]{0,1:T(8,128)(2,1)} %param.3) | data formatting | bytes 131072 | tf_op args[1]
  2.2 62.1 %shard_map.41 = (bf16[3,256,512]{2,1,0:T(8,128)(2,1)}, f32[256,64]{1,0:T(8,128)}) custom-call(bf16[512,4096]{1,0:T(8,128)(2,1)} %grads_hbm.1, bf16[512,64]{1,0:T(8,128)(2,1)} %copy.4.targ_hbm), custom_call_target="tpu_custom_call" | custom-call | tf_op jit(solution)/shard_map/pallas_call | solution.py:212
  64.3 1.6 %copy.5 = f32[256,64]{0,1:T(8,128)} copy(f32[256,64]{1,0:T(8,128)} %get-tuple-element.3) | data formatting | bytes 131072 | tf_op jit(solution)/shard_map/pallas_call | solution.py:212
  66.0 2.1 %copy.7 = bf16[3,256,512]{2,1,0:T(8,128)(2,1)} copy(bf16[3,256,512]{2,1,0:T(8,128)(2,1)} %get-tuple-element.6) | data formatting | bytes 1572864

commit v2 on v0

v2 whole, which is shorter than its diff:
```python
import functools

import jax
import jax.numpy as jnp
from jax import lax
from jax.experimental import pallas as pl
from jax.experimental.pallas import tpu as pltpu
from jax.sharding import PartitionSpec as P

MESH = pl.DeviceIdType.MESH
NT = (((1,), (1,)), ((), ()))
HALF_GROUPS = ((0, 128), (128, 64), (192, 64))
LAST_PIECES = 4
STEP = 1024
TURN = 128


def chunk_list(half, features):
    groups = [(h * half + start, rows) for h in range(2) for start, rows in HALF_GROUPS]
    chunks = []
    for index, (start, rows) in enumerate(groups):
        pieces = LAST_PIECES if index == len(groups) - 1 else 1
        width = features // pieces
        chunks.append([(start, rows, at * width, width) for at in range(pieces)])
    return groups, chunks


def kernel(
    scale,
    grads_hbm, targ_hbm, tiles, infl,
    right, left, targ_own, targ_chip, targ_far, targ_pass, self_out, self_in, self_keep,
    part_out, part_in, part_keep, staged, turned,
    in_sem, diag_sem, own_sem, targ_sem, left_send, chip_send, left_recv, right_recv,
    targ_send, targ_recv, self_send, self_recv, part_send, part_recv, res_send, res_recv, turn_send, turn_recv,
):
    rows, features = grads_hbm.shape
    half = rows // 2
    blk, y = lax.axis_index("blk"), lax.axis_index("tgt")
    core, z = lax.rem(blk, 2), lax.rem(blk // 2, 2)
    role = lax.rem(core + z, 2)
    lead, other_role = role == 1, role == 0
    chip = blk + 1 - 2 * core
    far = chip + 2 - 4 * z
    whose = chip + role * (far - chip)
    y_other = 1 - y
    groups, chunks = chunk_list(half, features)
    per_half = len(HALF_GROUPS)
    flat = [piece for pieces in chunks for piece in pieces]

    def there(block, side):
        return {"blk": block, "tgt": side}

    def half_of(side):
        return pl.ds(pl.multiple_of(side * half, half), half)

    def remote(source, target, send, recv, device):
        return pltpu.make_async_remote_copy(
            src_ref=source, dst_ref=target, send_sem=send, recv_sem=recv, device_id=device, device_id_type=MESH
        )

    def signal(sem, device):
        pl.semaphore_signal(sem, inc=1, device_id=device, device_id_type=MESH)

    load_own = pltpu.make_async_copy(grads_hbm, right.at[0], own_sem)
    load_own.start()
    load_targ = pltpu.make_async_copy(targ_hbm, targ_own, targ_sem)
    load_targ.start()

    barrier = pltpu.get_barrier_semaphore()

    @pl.when(lead)
    def _():
        signal(barrier, there(far, y))
        signal(barrier, there(chip, y))

    signal(barrier, there(blk, y_other))
    pl.semaphore_wait(barrier, 2)

    def left_copy(at, send, block):
        start, count, first, width = flat[at]
        where = (pl.ds(start, count), pl.ds(first, width))
        return remote(grads_hbm.at[where], left.at[where], send.at[at], left_recv.at[at], there(block, y))

    right_copy = remote(grads_hbm, right.at[1], chip_send.at[0], right_recv, there(chip, y))
    targ_to_chip = remote(targ_hbm, targ_chip, targ_send.at[0], targ_recv.at[0], there(chip, y))
    targ_to_far = remote(targ_chip, targ_far, targ_send.at[1], targ_recv.at[1], there(far, y))
    targ_to_pass = remote(targ_hbm, targ_pass, targ_send.at[2], targ_recv.at[2], there(far, y))
    targ_passed = remote(targ_pass, targ_far, targ_send.at[3], targ_recv.at[1], there(chip, y))

    @pl.when(lead)
    def _():
        for at in range(len(flat)):
            left_copy(at, left_send, far).start()
        targ_to_pass.start()

    signal(diag_sem, there(blk, y_other))

    @pl.when(other_role)
    def _():
        signal(in_sem, there(chip, y))
        right_copy.start()
        targ_to_chip.start()

    @pl.when(lead)
    def _():
        pl.semaphore_wait(in_sem, 1)
        for at in range(len(flat)):
            left_copy(at, chip_send, chip).start()
        targ_to_chip.start()

    def contract(lhs, rhs, first, width, init):
        def body(k, total):
            cols = pl.ds(pl.multiple_of(first + k * STEP, STEP), STEP)
            return total + lax.dot_general(lhs(cols), rhs(cols), NT, preferred_element_type=jnp.float32)

        return lax.fori_loop(0, width // STEP, body, init)

    load_own.wait()
    zero = jnp.zeros((128, half), jnp.float32)
    self_copy = remote(self_out, self_in, self_send, self_recv, there(blk, y_other))
    for into, side in ((self_out, y_other), (self_keep, y)):
        for r in range(half // 128):
            mine = pl.ds(pl.multiple_of(side * half + r * 128, 128), 128)
            for n in range(2):
                into[pl.ds(r * 128, 128), pl.ds(n * half, half)] = contract(
                    lambda cols: right[0, mine, cols],
                    lambda cols: right[0, pl.ds(n * half, half), cols],
                    0, features, zero,
                )
        if into is self_out:
            self_copy.start()

    part_copies = [
        remote(
            part_out.at[pl.ds(start, count)], part_in.at[pl.ds(start, count)],
            part_send.at[g], part_recv.at[g], there(blk, y_other),
        )
        for g, (start, count) in enumerate(groups)
    ]

    def res_copy(g, slot, side, block):
        start, count = groups[g]
        return remote(
            staged.at[pl.ds(start, count)],
            tiles.at[slot, pl.ds(start % half, count), half_of(side)],
            res_send.at[g], res_recv.at[slot - 1, side, g % per_half], there(block, g // per_half),
        )

    def turn_copy(n):
        cols = pl.ds(n * TURN, TURN)
        return remote(turned.at[:, cols], tiles.at[2, :, cols], turn_send.at[n], turn_recv.at[n], there(chip, y))

    def finish(g):
        start, count = groups[g]
        part_copies[g].wait_recv()
        here = pl.ds(start, count)
        staged[here, :] = ((part_keep[here, :] + part_in[here, :]) * scale).astype(jnp.bfloat16)
        res_copy(g, 1 + role, y, whose).start()
        end = start + count
        if end % TURN == 0:
            here = pl.ds(end - TURN, TURN)
            block = ((part_keep[here, :] + part_in[here, :]) * scale).T.astype(jnp.bfloat16)

            @pl.when(lead)
            def _():
                turned[:, end - TURN : end] = block
                turn_copy(end // TURN - 1).start()

            @pl.when(other_role)
            def _():
                tiles[1, :, end - TURN : end] = block

    @pl.when(lead)
    def _():
        targ_to_chip.wait_recv()
        targ_to_far.start()
        right_copy.wait_recv()

    pl.semaphore_wait(diag_sem, 1)
    at = 0
    for g, (start, count) in enumerate(groups):
        here = pl.ds(start, count)
        for piece, (_, _, first, width) in enumerate(chunks[g]):
            left_copy(at, left_send, far).wait_recv()
            at += 1
            for into, side in ((part_out, y_other), (part_keep, y)):
                into[here, :] = contract(
                    lambda cols: left[here, cols],
                    lambda cols: right[role, half_of(side), cols],
                    first, width,
                    jnp.zeros((count, half), jnp.float32) if piece == 0 else into[here, :],
                )
                if piece == len(chunks[g]) - 1 and into is part_out:
                    part_copies[g].start()
        if g >= 1:
            finish(g - 1)
        if g == 0:
            self_copy.wait_recv()
            tiles[0] = ((self_keep[...] + self_in[...]) * scale).astype(jnp.bfloat16)
    finish(len(groups) - 1)

    def influence_of(targets, slot):
        return lax.dot_general(targets[...], tiles[slot], NT, preferred_element_type=jnp.float32)

    @pl.when(lead)
    def _():
        targ_to_pass.wait_recv()
        targ_passed.start()
        for side in range(2):
            for g in range(per_half):
                res_copy(g, 1, side, whose).wait_recv()

    @pl.when(other_role)
    def _():
        targ_to_chip.wait_recv()

    load_targ.wait()
    infl[...] = influence_of(targ_own, 0) + influence_of(targ_chip, 1)
    targ_to_far.wait_recv()

    @pl.when(lead)
    def _():
        for side in range(2):
            for g in range(per_half):
                res_copy(g, 2, side, whose).wait_recv()

    @pl.when(other_role)
    def _():
        for n in range(rows // TURN):
            turn_copy(n).wait_recv()

    infl[...] += influence_of(targ_far, 2)

    for g in range(len(groups)):
        part_copies[g].wait_send()
        res_copy(g, 1 + role, y, whose).wait_send()
    self_copy.wait_send()
    targ_to_chip.wait_send()

    @pl.when(lead)
    def _():
        for at in range(len(flat)):
            left_copy(at, left_send, far).wait_send()
            left_copy(at, chip_send, chip).wait_send()
        for copy in (targ_to_far, targ_to_pass, targ_passed):
            copy.wait_send()
        for n in range(rows // TURN):
            turn_copy(n).wait_send()

    @pl.when(other_role)
    def _():
        right_copy.wait_send()


def put_kernel(tiles, infl, tiles_hbm, infl_hbm, sems):
    puts = [pltpu.make_async_copy(infl, infl_hbm, sems.at[3])]
    puts += [pltpu.make_async_copy(tiles.at[slot], tiles_hbm.at[slot], sems.at[slot]) for slot in range(3)]
    for put in puts:
        put.start()
    for put in puts:
        put.wait()


def per_device(gradients, targets):
    rows, features = gradients.shape
    half, columns = rows // 2, targets.shape[1]
    groups, chunks = chunk_list(half, features)
    count = sum(len(pieces) for pieces in chunks)
    bf16, f32 = jnp.bfloat16, jnp.float32
    dma, vmem = pltpu.SemaphoreType.DMA, pltpu.VMEM
    shapes = (jax.ShapeDtypeStruct((3, half, rows), bf16), jax.ShapeDtypeStruct((columns, half), f32))
    tiles, infl = pl.pallas_call(
        functools.partial(kernel, 1.0 / (2 * features) ** 0.5),
        out_shape=shapes,
        in_specs=[pl.BlockSpec(memory_space=pltpu.HBM)] * 2,
        out_specs=[pl.BlockSpec(memory_space=vmem)] * 2,
        scratch_shapes=[
            vmem((2, rows, features), bf16),
            vmem((rows, features), bf16),
            *[vmem((columns, rows), bf16)] * 4,
            *[vmem((half, rows), f32)] * 3,
            *[vmem((rows, half), f32)] * 3,
            vmem((rows, half), bf16),
            vmem((half, rows), bf16),
            pltpu.SemaphoreType.REGULAR, pltpu.SemaphoreType.REGULAR,
            dma, dma, dma((count,)), dma((count,)), dma((count,)), dma,
            dma((4,)), dma((3,)), dma, dma,
            dma((len(groups),)), dma((len(groups),)), dma((len(groups),)), dma((2, 2, len(HALF_GROUPS))),
            dma((rows // TURN,)), dma((rows // TURN,)),
        ],
        compiler_params=pltpu.CompilerParams(
            collective_id=0, has_side_effects=True, vmem_limit_bytes=48 * 2**20
        ),
    )(pltpu.with_memory_space_constraint(gradients, pltpu.HBM), pltpu.with_memory_space_constraint(targets.T, pltpu.HBM))
    tiles, infl = pl.pallas_call(
        put_kernel,
        out_shape=shapes,
        in_specs=[pl.BlockSpec(memory_space=vmem)] * 2,
        out_specs=[pl.BlockSpec(memory_space=pltpu.HBM)] * 2,
        scratch_shapes=[dma((4,))],
        compiler_params=pltpu.CompilerParams(vmem_limit_bytes=16 * 2**20),
    )(tiles, infl)
    return tiles, infl.T


def solution(mesh):
    placed = (P("blk", "tgt"), P("blk", None))
    return jax.shard_map(
        per_device,
        mesh=mesh,
        in_specs=placed,
        out_specs=(P(None, ("blk", "tgt"), None), P(("blk", "tgt"), None)),
        check_vma=False,
    )
```

time: 159 us -> 59.8 us (0.38)
  the two profiles are of different devices: /device:TPU:1 before, /device:TPU:93 now
where the time goes in v2:
time: 59.8 us; the launch traced here: 59.7 us
  Pallas kernels  59.1 us (99%)
  between operations  0.64 us (1%)
    pallas_call x1, Pallas kernels, per_device(): pl.pallas_call(functools.partial(kernel, 1.0 / (2 * features) ** 0.5), ou...  58.1 us

profile of v2, /device:TPU:93, one launch (start us, length us, event | category | flops | bytes accessed | tf_op | source)
XLA Modules:
  0.0 59.7 jit_solution(11454796398899317090)
XLA Ops:
  0.6 58.1 %shard_map.41 = (bf16[3,256,512]{2,1,0:T(8,128)(2,1)S(1)}, f32[64,256]{1,0:T(8,128)S(1)}) custom-call(bf16[512,4096]{1,0:T(8,128)(2,1)} %grads_hbm.1, bf16[64,512]{1,0:T(8,128)(2,1)} %bitcast.2), custom_call_target="tpu_custom_call" | custom-call | tf_op jit(solution)/shard_map/pallas_call | solution.py:272
  58.8 0.9 %shard_map.42 = (bf16[3,256,512]{2,1,0:T(8,128)(2,1)}, f32[64,256]{1,0:T(8,128)}) custom-call(bf16[3,256,512]{2,1,0:T(8,128)(2,1)S(1)} %get-tuple-element.6.tiles, f32[64,256]{1,0:T(8,128)S(1)} %get-tuple-element.7.infl), custom_call_target="tpu_custom_call" | custom-call | tf_op jit(solution)/shard_map/pallas_call | solution.py:295

commit v3 on v2

v3 whole, which is shorter than its diff:
```python
import functools

import jax
import jax.numpy as jnp
from jax import lax
from jax.experimental import pallas as pl
from jax.experimental.pallas import tpu as pltpu
from jax.sharding import PartitionSpec as P

MESH = pl.DeviceIdType.MESH
NT = (((1,), (1,)), ((), ()))
GROUPS = ((0, 128), (128, 128), (256, 128), (384, 96), (480, 32))
LAST_PIECES = 4
STEP = 1024
TURN = 128


def chunk_list(features):
    chunks = []
    for index, (start, rows) in enumerate(GROUPS):
        pieces = LAST_PIECES if index == len(GROUPS) - 1 else 1
        width = features // pieces
        chunks.append([(start, rows, at * width, width) for at in range(pieces)])
    return chunks


def kernel(
    scale,
    grads_hbm, targ_hbm, tiles, infl,
    right, left, targ_own, targ_chip, targ_far, targ_pass, self_out, self_in, self_keep,
    part_out, part_in, part_keep, staged, last_out, last_in, last_staged, turned,
    in_sem, diag_sem, own_sem, targ_sem, left_send, chip_send, left_recv, right_recv,
    targ_send, targ_recv, self_send, self_recv, part_send, part_recv, res_send, res_recv, turn_send, turn_recv,
):
    rows, features = grads_hbm.shape
    half = rows // 2
    blk, y = lax.axis_index("blk"), lax.axis_index("tgt")
    core, z = lax.rem(blk, 2), lax.rem(blk // 2, 2)
    lead, near = core == 1, core == 0
    streams = lax.rem(core + z, 2) == 1
    lends, borrows = core + z == 0, core - z == 1
    odd_near, odd_lead = z - core == 1, z + core == 2
    chip = blk + 1 - 2 * core
    across = blk - core + 2 - 4 * z
    whose = chip + core * (across + z - chip)
    right_at = core * (1 - z)
    made = 1 + core
    y_other = 1 - y
    groups, chunks, final = GROUPS, chunk_list(features), len(GROUPS) - 1
    flat = [piece for pieces in chunks for piece in pieces]

    def there(block, side):
        return {"blk": block, "tgt": side}

    def half_of(side):
        return pl.ds(pl.multiple_of(side * half, half), half)

    def remote(source, target, send, recv, device):
        return pltpu.make_async_remote_copy(
            src_ref=source, dst_ref=target, send_sem=send, recv_sem=recv, device_id=device, device_id_type=MESH
        )

    def signal(sem, device):
        pl.semaphore_signal(sem, inc=1, device_id=device, device_id_type=MESH)

    load_own = pltpu.make_async_copy(grads_hbm, right.at[0], own_sem)
    load_own.start()
    load_targ = pltpu.make_async_copy(targ_hbm, targ_own, targ_sem)
    load_targ.start()

    barrier = pltpu.get_barrier_semaphore()

    signal(barrier, there(blk, y_other))

    @pl.when(jnp.logical_not(lends))
    def _():
        signal(barrier, there(across + 1, y))

    @pl.when(borrows)
    def _():
        signal(barrier, there(across, y))
        signal(barrier, there(chip, y))

    @pl.when(z == 1)
    def _():
        signal(barrier, there(chip, y))

    pl.semaphore_wait(barrier, 3 - (1 - core) * (1 - z))

    def left_copy(at, send, block):
        start, count, first, width = flat[at]
        where = (pl.ds(start, count), pl.ds(first, width))
        return remote(grads_hbm.at[where], left.at[where], send.at[at], left_recv.at[at], there(block, y))

    right_copy = remote(grads_hbm, right.at[1], chip_send.at[0], right_recv, there(chip, y))
    targ_to_chip = remote(targ_hbm, targ_chip, targ_send.at[0], targ_recv.at[0], there(chip, y))
    targ_to_far = remote(targ_hbm, targ_far, targ_send.at[1], targ_recv.at[1], there(across + 1, y))
    targ_lent = remote(targ_chip, targ_far, targ_send.at[2], targ_recv.at[1], there(across, y))
    targ_to_pass = remote(targ_hbm, targ_pass, targ_send.at[2], targ_recv.at[2], there(across + 1, y))
    targ_passed = remote(targ_pass, targ_far, targ_send.at[3], targ_recv.at[1], there(chip, y))

    @pl.when(streams)
    def _():
        for at in range(len(flat)):
            left_copy(at, left_send, across + 1).start()

    @pl.when(borrows)
    def _():
        targ_to_far.start()
        pl.semaphore_wait(in_sem, 1)

    @pl.when(odd_near)
    def _():
        targ_to_pass.start()

    signal(diag_sem, there(blk, y_other))

    @pl.when(lends)
    def _():
        signal(in_sem, there(chip, y))
        right_copy.start()

    @pl.when(lead)
    def _():
        for at in range(len(flat)):
            left_copy(at, chip_send, chip).start()

    targ_to_chip.start()

    def contract(lhs, rhs, first, width, init):
        def body(k, total):
            cols = pl.ds(pl.multiple_of(first + k * STEP, STEP), STEP)
            return total + lax.dot_general(lhs(cols), rhs(cols), NT, preferred_element_type=jnp.float32)

        return lax.fori_loop(0, width // STEP, body, init)

    load_own.wait()
    zero = jnp.zeros((128, half), jnp.float32)
    self_copy = remote(self_out, self_in, self_send, self_recv, there(blk, y_other))
    for into, side in ((self_out, y_other), (self_keep, y)):
        for r in range(half // 128):
            mine = pl.ds(pl.multiple_of(side * half + r * 128, 128), 128)
            for n in range(2):
                into[pl.ds(r * 128, 128), pl.ds(n * half, half)] = contract(
                    lambda cols: right[0, mine, cols],
                    lambda cols: right[0, pl.ds(n * half, half), cols],
                    0, features, zero,
                )
        if into is self_out:
            self_copy.start()

    part_copies = [
        remote(
            part_out.at[pl.ds(start, count)], part_in.at[pl.ds(start, count)],
            part_send.at[g], part_recv.at[g], there(blk, y_other),
        )
        for g, (start, count) in enumerate(groups[:final])
    ]
    part_copies.append(remote(last_out, last_in, part_send.at[final], part_recv.at[final], there(blk, y_other)))

    def res_copy(g, slot, side):
        start, count = groups[g]
        return remote(
            staged.at[pl.ds(start, count)],
            tiles.at[slot, pl.ds(start % half, count), half_of(side)],
            res_send.at[g], res_recv.at[slot - 1, side, g], there(whose, start // half),
        )

    def last_res_copy(slot):
        start, count = groups[final]
        return remote(
            last_staged, tiles.at[slot, pl.ds(start % half, count), :],
            res_send.at[final], res_recv.at[slot - 1, 0, final], there(whose, start // half),
        )

    holds_last = y == groups[final][0] // half

    def wait_results(slot):
        for g, (start, _) in enumerate(groups):
            @pl.when(y == start // half)
            def _():
                if g == final:
                    last_res_copy(slot).wait_recv()
                else:
                    for side in range(2):
                        res_copy(g, slot, side).wait_recv()

    def turn_copy(n):
        cols = pl.ds(n * TURN, TURN)
        return remote(turned.at[:, cols], tiles.at[2, :, cols], turn_send.at[n], turn_recv.at[n], there(chip, y))

    def finish(g):
        start, count = groups[g]
        end = start + count
        here = pl.ds(start, count)
        part_copies[g].wait_recv()
        if g < final:
            summed = (part_keep[here, :] + part_in[here, :]) * scale
            part_keep[here, :] = summed
            staged[here, :] = summed.astype(jnp.bfloat16)

            @pl.when(near)
            def _():
                res_copy(g, made, y).start()
        else:
            @pl.when(holds_last)
            def _():
                last_staged[...] = ((last_out[...] + last_in[...]) * scale).astype(jnp.bfloat16)
                last_res_copy(made).start()

            part_keep[here, :] = (last_out[:, half_of(y)] + last_in[:, half_of(y)]) * scale
        if end % TURN == 0:
            block = part_keep[end - TURN : end, :].T.astype(jnp.bfloat16)

            @pl.when(borrows)
            def _():
                turned[:, end - TURN : end] = block
                turn_copy(end // TURN - 1).start()

            @pl.when(jnp.logical_not(borrows))
            def _():
                tiles[made, :, end - TURN : end] = block

    def influence_of(targets, slot):
        return lax.dot_general(targets[...], tiles[slot], NT, preferred_element_type=jnp.float32)

    def near_influence():
        infl[...] = influence_of(targ_own, 0) + influence_of(targ_chip, 1)

    targ_to_chip.wait_recv()

    @pl.when(borrows)
    def _():
        targ_lent.start()
        right_copy.wait_recv()

    load_targ.wait()
    pl.semaphore_wait(diag_sem, 1)
    at = 0
    for g, (start, count) in enumerate(groups):
        here = pl.ds(start, count)
        if g == final:
            @pl.when(lead)
            def _():
                wait_results(1)
                near_influence()
        for piece, (_, _, first, width) in enumerate(chunks[g]):
            if g == final and piece == 1:
                @pl.when(lead)
                def _():
                    for early in range(final - 1):
                        res_copy(early, made, y).start()

            left_copy(at, left_send, across + 1).wait_recv()
            at += 1
            if g == final:
                for n in range(2):
                    cols = pl.ds(n * half, half)
                    last_out[:, cols] = contract(
                        lambda k: left[here, k],
                        lambda k: right[right_at, cols, k],
                        first, width,
                        jnp.zeros((count, half), jnp.float32) if piece == 0 else last_out[:, cols],
                    )
                if piece == len(chunks[g]) - 1:
                    part_copies[g].start()
                continue
            for into, side in ((part_out, y_other), (part_keep, y)):
                into[here, :] = contract(
                    lambda k: left[here, k],
                    lambda k: right[right_at, half_of(side), k],
                    first, width, jnp.zeros((count, half), jnp.float32),
                )
                if into is part_out:
                    part_copies[g].start()
        if g >= 1:
            finish(g - 1)
        if g == 0:
            self_copy.wait_recv()
            tiles[0] = ((self_keep[...] + self_in[...]) * scale).astype(jnp.bfloat16)

    @pl.when(lead)
    def _():
        res_copy(final - 1, made, y).start()

    @pl.when(odd_lead)
    def _():
        targ_to_far.start()

    @pl.when(borrows)
    def _():
        targ_to_pass.wait_recv()
        targ_passed.start()

    finish(final)

    @pl.when(near)
    def _():
        near_influence()

    targ_to_far.wait_recv()

    @pl.when(streams)
    def _():
        wait_results(2)

    @pl.when(lends)
    def _():
        for n in range(rows // TURN):
            turn_copy(n).wait_recv()

    infl[...] += influence_of(targ_far, 2)

    for g in range(len(groups)):
        part_copies[g].wait_send()
        if g < final:
            res_copy(g, made, y).wait_send()

    @pl.when(holds_last)
    def _():
        last_res_copy(made).wait_send()

    self_copy.wait_send()
    targ_to_chip.wait_send()

    @pl.when(streams)
    def _():
        for at in range(len(flat)):
            left_copy(at, left_send, across + 1).wait_send()

    @pl.when(lead)
    def _():
        for at in range(len(flat)):
            left_copy(at, chip_send, chip).wait_send()
        targ_to_far.wait_send()

    @pl.when(borrows)
    def _():
        targ_lent.wait_send()
        targ_passed.wait_send()
        for n in range(rows // TURN):
            turn_copy(n).wait_send()

    @pl.when(odd_near)
    def _():
        targ_to_pass.wait_send()

    @pl.when(lends)
    def _():
        right_copy.wait_send()


def put_kernel(tiles, infl, tiles_hbm, infl_hbm, sems):
    puts = [pltpu.make_async_copy(infl, infl_hbm, sems.at[3])]
    puts += [pltpu.make_async_copy(tiles.at[slot], tiles_hbm.at[slot], sems.at[slot]) for slot in range(3)]
    for put in puts:
        put.start()
    for put in puts:
        put.wait()


def per_device(gradients, targets):
    rows, features = gradients.shape
    half, columns = rows // 2, targets.shape[1]
    count = sum(len(pieces) for pieces in chunk_list(features))
    last, groups = GROUPS[-1][1], len(GROUPS)
    bf16, f32 = jnp.bfloat16, jnp.float32
    dma, vmem = pltpu.SemaphoreType.DMA, pltpu.VMEM
    shapes = (jax.ShapeDtypeStruct((3, half, rows), bf16), jax.ShapeDtypeStruct((columns, half), f32))
    tiles, infl = pl.pallas_call(
        functools.partial(kernel, 1.0 / (2 * features) ** 0.5),
        out_shape=shapes,
        in_specs=[pl.BlockSpec(memory_space=pltpu.HBM)] * 2,
        out_specs=[pl.BlockSpec(memory_space=vmem)] * 2,
        scratch_shapes=[
            vmem((2, rows, features), bf16),
            vmem((rows, features), bf16),
            *[vmem((columns, rows), bf16)] * 4,
            *[vmem((half, rows), f32)] * 3,
            *[vmem((rows, half), f32)] * 3,
            vmem((rows, half), bf16),
            vmem((last, rows), f32), vmem((last, rows), f32), vmem((last, rows), bf16),
            vmem((half, rows), bf16),
            pltpu.SemaphoreType.REGULAR, pltpu.SemaphoreType.REGULAR,
            dma, dma, dma((count,)), dma((count,)), dma((count,)), dma,
            dma((4,)), dma((3,)), dma, dma,
            dma((groups,)), dma((groups,)), dma((groups,)), dma((2, 2, groups)),
            dma((rows // TURN,)), dma((rows // TURN,)),
        ],
        compiler_params=pltpu.CompilerParams(
            collective_id=0, has_side_effects=True, vmem_limit_bytes=48 * 2**20
        ),
    )(pltpu.with_memory_space_constraint(gradients, pltpu.HBM), pltpu.with_memory_space_constraint(targets.T, pltpu.HBM))
    tiles, infl = pl.pallas_call(
        put_kernel,
        out_shape=shapes,
        in_specs=[pl.BlockSpec(memory_space=vmem)] * 2,
        out_specs=[pl.BlockSpec(memory_space=pltpu.HBM)] * 2,
        scratch_shapes=[dma((4,))],
        compiler_params=pltpu.CompilerParams(vmem_limit_bytes=16 * 2**20),
    )(tiles, infl)
    return tiles, infl.T


def solution(mesh):
    placed = (P("blk", "tgt"), P("blk", None))
    return jax.shard_map(
        per_device,
        mesh=mesh,
        in_specs=placed,
        out_specs=(P(None, ("blk", "tgt"), None), P(("blk", "tgt"), None)),
        check_vma=False,
    )
```

time: 59.8 us -> 59.1 us (0.988)
  the two profiles are of different devices: /device:TPU:93 before, /device:TPU:1 now
where the time goes in v3:
time: 59.1 us; the launch traced here: 59 us
  Pallas kernels  58.3 us (99%)
  between operations  0.64 us (1%)
    pallas_call x1, Pallas kernels, per_device(): pl.pallas_call(functools.partial(kernel, 1.0 / (2 * features) ** 0.5), ou...  57.4 us

profile of v3, /device:TPU:1, one launch (start us, length us, event | category | flops | bytes accessed | tf_op | source)
XLA Modules:
  0.0 59.0 jit_solution(12044842871655850512)
XLA Ops:
  0.6 57.4 %shard_map.41 = (bf16[3,256,512]{2,1,0:T(8,128)(2,1)S(1)}, f32[64,256]{1,0:T(8,128)S(1)}) custom-call(bf16[512,4096]{1,0:T(8,128)(2,1)} %grads_hbm.1, bf16[64,512]{1,0:T(8,128)(2,1)} %bitcast.2), custom_call_target="tpu_custom_call" | custom-call | tf_op jit(solution)/shard_map/pallas_call | solution.py:370
  58.0 0.9 %shard_map.42 = (bf16[3,256,512]{2,1,0:T(8,128)(2,1)}, f32[64,256]{1,0:T(8,128)}) custom-call(bf16[3,256,512]{2,1,0:T(8,128)(2,1)S(1)} %get-tuple-element.6.tiles, f32[64,256]{1,0:T(8,128)S(1)} %get-tuple-element.7.infl), custom_call_target="tpu_custom_call" | custom-call | tf_op jit(solution)/shard_map/pallas_call | solution.py:394

commit v4 on v3

--- a/solution.py
+++ b/solution.py
@@ -156,7 +156,11 @@
         )
         for g, (start, count) in enumerate(groups[:final])
     ]
-    part_copies.append(remote(last_out, last_in, part_send.at[final], part_recv.at[final], there(blk, y_other)))
+    for n in range(2):
+        cols = (slice(None), pl.ds(n * half, half))
+        part_copies.append(
+            remote(last_out.at[cols], last_in.at[cols], part_send.at[final + n], part_recv.at[final + n], there(blk, y_other))
+        )
 
     def res_copy(g, slot, side):
         start, count = groups[g]
@@ -193,7 +197,8 @@
         start, count = groups[g]
         end = start + count
         here = pl.ds(start, count)
-        part_copies[g].wait_recv()
+        for copy in part_copies[g : g + 1] if g < final else part_copies[final:]:
+            copy.wait_recv()
         if g < final:
             summed = (part_keep[here, :] + part_in[here, :]) * scale
             part_keep[here, :] = summed
@@ -262,8 +267,8 @@
                         first, width,
                         jnp.zeros((count, half), jnp.float32) if piece == 0 else last_out[:, cols],
                     )
-                if piece == len(chunks[g]) - 1:
-                    part_copies[g].start()
+                    if piece == len(chunks[g]) - 1:
+                        part_copies[g + n].start()
                 continue
             for into, side in ((part_out, y_other), (part_keep, y)):
                 into[here, :] = contract(
@@ -311,10 +316,10 @@
 
     infl[...] += influence_of(targ_far, 2)
 
-    for g in range(len(groups)):
-        part_copies[g].wait_send()
-        if g < final:
-            res_copy(g, made, y).wait_send()
+    for copy in part_copies:
+        copy.wait_send()
+    for g in range(final):
+        res_copy(g, made, y).wait_send()
 
     @pl.when(holds_last)
     def _():
@@ -384,7 +389,7 @@
             pltpu.SemaphoreType.REGULAR, pltpu.SemaphoreType.REGULAR,
             dma, dma, dma((count,)), dma((count,)), dma((count,)), dma,
             dma((4,)), dma((3,)), dma, dma,
-            dma((groups,)), dma((groups,)), dma((groups,)), dma((2, 2, groups)),
+            dma((groups + 1,)), dma((groups + 1,)), dma((groups,)), dma((2, 2, groups)),
             dma((rows // TURN,)), dma((rows // TURN,)),
         ],
         compiler_params=pltpu.CompilerParams(

time: 59.1 us -> 59.1 us (level)
  no operation moved by 1% of the time
where the time goes in v4:
time: 59.1 us; the launch traced here: 59 us
  Pallas kernels  58.4 us (99%)
  between operations  0.64 us (1%)
    pallas_call x1, Pallas kernels, per_device(): pl.pallas_call(functools.partial(kernel, 1.0 / (2 * features) ** 0.5), ou...  57.4 us

profile of v4, /device:TPU:1, one launch (start us, length us, event | category | flops | bytes accessed | tf_op | source)
XLA Modules:
  0.0 59.0 jit_solution(17594274473024985740)
XLA Ops:
  0.6 57.4 %shard_map.41 = (bf16[3,256,512]{2,1,0:T(8,128)(2,1)S(1)}, f32[64,256]{1,0:T(8,128)S(1)}) custom-call(bf16[512,4096]{1,0:T(8,128)(2,1)} %grads_hbm.1, bf16[64,512]{1,0:T(8,128)(2,1)} %bitcast.2), custom_call_target="tpu_custom_call" | custom-call | tf_op jit(solution)/shard_map/pallas_call | solution.py:375
  58.1 0.9 %shard_map.42 = (bf16[3,256,512]{2,1,0:T(8,128)(2,1)}, f32[64,256]{1,0:T(8,128)}) custom-call(bf16[3,256,512]{2,1,0:T(8,128)(2,1)S(1)} %get-tuple-element.6.tiles, f32[64,256]{1,0:T(8,128)S(1)} %get-tuple-element.7.infl), custom_call_target="tpu_custom_call" | custom-call | tf_op jit(solution)/shard_map/pallas_call | solution.py:399
